TPU v7x, 256 devices: a whole 4x4x8 slice. The times are simulated.
256 devices in a mesh: freq: 32 (over z, x_hi, core), rec: 8 (over y, x_lo).
Axes of the slice: x: 4 (x_hi: 2, x_lo: 2; x = x_hi * 2 + x_lo), y: 4, z: 8, core: 2. Of those that a mesh axis runs over, the one named last changes fastest.
Arguments:
- kernel: bfloat16 [2, 128, 256, 9216], P(None, 'freq', None, 'rec'), may hold values from -0.09375 to 0.09375
- focusing_in: bfloat16 [64, 9216, 1024], P('freq', 'rec'), may hold values from -6 to 6
- onset_src: int32 [64, 256], P('freq'), may hold values from 128 to 895
- onset_rec: int32 [64, 9216], P('freq', 'rec'), may hold values from 128 to 895
Outputs:
- focusing: bfloat16 [64, 9216, 1024], P('freq', 'rec')
- upgoing_field: bfloat16 [64, 256, 1024], P('freq', 'rec')
All inputs are finite; a program needn't handle non-finite values.
Results may differ from a plain program's by a relative error of at most 0.018.
Values may be sent and summed in bfloat16 or wider, within the bound.
No kernel may reach another device: no remote copies, remote signals or barrier semaphores. Data moves between devices by JAX's collectives and lax.ppermute only.
A program may use at most 64 MiB of HBM per device.

v0:
```python
import jax
import jax.numpy as jnp
from jax import lax
from jax.sharding import PartitionSpec as P

LOW = 8
ITERS = 2


def make_tables(count, samples, lowest):
    freqs = (lax.iota(jnp.int32, count) + lowest)[:, None]
    times = lax.iota(jnp.int32, samples)[None, :]
    phase = (freqs * times % samples).astype(jnp.float32) * (2.0 * 3.141592653589793 / samples)
    both = jnp.stack([jnp.cos(phase), -jnp.sin(phase)])
    forward = both.astype(jnp.bfloat16)
    inverse = (forward.astype(jnp.float32) * (2.0 / samples)).astype(jnp.bfloat16)
    return (forward, inverse)


def forward_mdc(block_slice, spread_layout):
    real = jnp.einsum(
        "wch,wah->cwa", block_slice[0], spread_layout[0], preferred_element_type=jnp.float32
    ) - jnp.einsum(
        "wch,wah->cwa", block_slice[1], spread_layout[1], preferred_element_type=jnp.float32
    )
    imag = jnp.einsum(
        "wch,wah->cwa", block_slice[0], spread_layout[1], preferred_element_type=jnp.float32
    ) + jnp.einsum(
        "wch,wah->cwa", block_slice[1], spread_layout[0], preferred_element_type=jnp.float32
    )
    return jnp.stack([real, imag], axis=1)


def adjoint_mdc(block_slice, piece_portion):
    real = jnp.einsum(
        "thl,htv->tvl", block_slice[0], piece_portion[:, 0], preferred_element_type=jnp.float32
    ) + jnp.einsum(
        "thl,htv->tvl", block_slice[1], piece_portion[:, 1], preferred_element_type=jnp.float32
    )
    imag = jnp.einsum(
        "thl,htv->tvl", block_slice[0], piece_portion[:, 1], preferred_element_type=jnp.float32
    ) - jnp.einsum(
        "thl,htv->tvl", block_slice[1], piece_portion[:, 0], preferred_element_type=jnp.float32
    )
    return jnp.stack([real, imag])


def body(kernel, focusing_in, onset_src, onset_rec):
    freq_count = lax.axis_size("freq")
    rec_count = lax.axis_size("rec")
    band = kernel.shape[1] * freq_count
    samples = focusing_in.shape[2]
    sources = kernel.shape[2]
    share = sources // rec_count
    forward, inverse = make_tables(band, samples, LOW)
    times = lax.iota(jnp.int32, samples)
    keep_rec = times[None, None, :] < onset_rec[:, :, None]
    first = lax.axis_index("rec") * share
    focusing = focusing_in
    upgoing_field = None
    for step in range(ITERS):
        spectrum = jnp.einsum(
            "prt,ckt->ckpr", focusing, forward, preferred_element_type=jnp.float32
        ).astype(jnp.bfloat16)
        spread_layout = lax.all_to_all(spectrum, "freq", split_axis=1, concat_axis=2, tiled=True)
        own_onsets = lax.dynamic_slice_in_dim(onset_src, first, share, 1)
        keep_src = times[None, None, :] < own_onsets[:, :, None]
        local = lax.psum_scatter(
            forward_mdc(kernel, spread_layout).astype(jnp.bfloat16),
            "rec",
            scatter_dimension=0,
            tiled=True,
        )
        series = lax.all_to_all(local, "freq", split_axis=3, concat_axis=2, tiled=True)
        signal = jnp.einsum("sckp,ckt->pst", series, inverse, preferred_element_type=jnp.float32)
        upgoing_field = signal.astype(jnp.bfloat16)
        muted = jnp.where(keep_src, signal, 0.0).astype(jnp.bfloat16)
        echo = jnp.einsum(
            "pst,ckt->sckp", muted, forward, preferred_element_type=jnp.float32
        ).astype(jnp.bfloat16)
        returned_output = lax.all_to_all(echo, "freq", split_axis=2, concat_axis=3, tiled=True)
        reflected = adjoint_mdc(kernel, lax.all_gather(returned_output, "rec", axis=0, tiled=True))
        reflected = reflected.astype(jnp.bfloat16)
        arrived = lax.all_to_all(reflected, "freq", split_axis=2, concat_axis=1, tiled=True)
        update = jnp.einsum("ckpr,ckt->prt", arrived, inverse, preferred_element_type=jnp.float32)
        focusing = (focusing_in.astype(jnp.float32) + jnp.where(keep_rec, update, 0.0)).astype(
            jnp.bfloat16
        )
    return (focusing, upgoing_field)


def solution(mesh):
    placed = (
        P(None, "freq", None, "rec"),
        P("freq", "rec", None),
        P("freq", None),
        P("freq", "rec"),
    )
    return jax.shard_map(
        body,
        mesh=mesh,
        in_specs=placed,
        out_specs=(P("freq", "rec", None), P("freq", "rec", None)),
        check_vma=False,
    )
```

profile of v0, /device:TPU:1, one launch (start us, length us, event | category | flops | bytes accessed | tf_op | source)
XLA Modules:
  0.0 511.5 jit_solution(12522489238005167587)
XLA Ops:
  7.2 2.4 cosine_convert_fusion
  9.7 3.8 fusion.6
  14.7 45.1 %all_to_all.138 = bf16[2,128,2,1152]{3,2,0,1:T(2,128)(2,1)S(1)} all-to-all(bf16[2,128,2,1152]{3,2,0,1:T(2,128)(2,1)S(1)} %copy.54), channel_id=1, replica_groups=mesh['freq'=32,'rec'=8] {'freq'}, dimensions={1} | all-to-all | bytes 2359296 | tf_op jit(solution)/shard_map/all_to_all | solution.py:65
  61.9 2.6 fusion.30
  64.6 2.5 fusion.28
  67.1 2.5 fusion.78
  72.9 70.0 %all-reduce.5.cloned.1.call-done = bf16[256,2,4,64]{3,2,1,0:T(4,128)(2,1)} async-done(((bf16[256,2,4,64]{3,2,1,0:T(4,128)(2,1)}), bf16[256,2,4,64]{3,2,1,0:T(4,128)(2,1)}) %all-reduce.5.cloned.1.call-update) | async-done | bytes 262160
  144.6 15.2 %all-to-all-start.1 = ((bf16[32,2,256]{2,1,0:T(2,128)(2,1)}), bf16[32,2,256]{2,1,0:T(2,128)(2,1)S(1)}, u32[]{:S(2)}, u32[]{:S(2)}) async-start(bf16[32,2,256]{2,1,0:T(2,128)(2,1)} %reshape.130), calls=%async_computation.1 | async-start | bytes 65536 | tf_op jit(solution)/shard_map/all_to_all | solution.py:74
  160.0 9.5 %all-to-all-done.1 = bf16[32,2,256]{2,1,0:T(2,128)(2,1)S(1)} async-done(((bf16[32,2,256]{2,1,0:T(2,128)(2,1)}), bf16[32,2,256]{2,1,0:T(2,128)(2,1)S(1)}, u32[]{:S(2)}, u32[]{:S(2)}) %all-to-all-start.1) | async-done | bytes 32800 | tf_op jit(solution)/shard_map/all_to_all | solution.py:74
  170.4 12.8 %all_to_all.139 = bf16[32,2,256]{2,1,0:T(2,128)(2,1)S(1)} all-to-all(bf16[32,2,256]{2,1,0:T(2,128)(2,1)S(1)} %reshape.132), channel_id=1, replica_groups=mesh['freq'=32,'rec'=8] {'freq'}, dimensions={0} | all-to-all | bytes 65536 | tf_op jit(solution)/shard_map/all_to_all | solution.py:81
  183.6 24.7 %all_gather.6 = bf16[256,2,4,64]{3,2,1,0:T(4,128)(2,1)S(1)} all-gather(bf16[32,2,4,64]{3,2,1,0:T(4,128)(2,1)S(1)} %copy.63), channel_id=1, replica_groups=mesh['freq'=32,'rec'=8] {'rec'}, dimensions={0}, use_global_device_ids=true | all-gather | bytes 294912 | tf_op jit(solution)/shard_map/all_gather | solution.py:82
  217.1 41.4 %all_to_all.140 = bf16[2,4,64,1152]{3,1,0,2:T(4,128)(2,1)S(1)} all-to-all(bf16[2,4,64,1152]{3,1,0,2:T(4,128)(2,1)S(1)} %copy.66), channel_id=1, replica_groups=mesh['freq'=32,'rec'=8] {'freq'}, dimensions={2} | all-to-all | bytes 2359296 | tf_op jit(solution)/shard_map/all_to_all | solution.py:84
  259.5 5.4 %fusion.9 = bf16[2,128,2,1152]{3,1,2,0:T(8,128)(2,1)S(1)} fusion(bf16[2,1152,1024]{2,1,0:T(8,128)(2,1)} %param.5, s32[2,1152]{1,0:T(2,128)S(1)} %copy-done.1, bf16[2,128,2,1152]{3,2,1,0:T(2,128)(2,1)S(1)} %bitcast.248, bf16[1,128,1024]{2,1,0:T(8,128)(2,1)S(1)} %get-tuple-element.11, bf16[1,128,1024]{2,1,0:T(8,128)(2,1)S(1)} %get-tuple-element.10), kind=kOutput, calls=%fused_computation.12 | convolution fusion | flops 2430402560 | bytes 7611392 | tf_op jit(solution)/shard_map/prt,ckt->ckpr/dot_general | solution.py:62
  266.1 36.5 %all_to_all.141 = bf16[2,128,2,1152]{3,2,0,1:T(2,128)(2,1)S(1)} all-to-all(bf16[2,128,2,1152]{3,2,0,1:T(2,128)(2,1)S(1)} %copy.69), channel_id=1, replica_groups=mesh['freq'=32,'rec'=8] {'freq'}, dimensions={1} | all-to-all | bytes 2359296 | tf_op jit(solution)/shard_map/all_to_all | solution.py:65
  304.5 2.5 fusion.24
  307.2 2.5 fusion.22
  309.7 2.5 fusion.84
  312.3 2.5 fusion.87
  315.9 69.1 %all-reduce.7.cloned.1.call-done = bf16[256,2,4,64]{3,2,1,0:T(4,128)(2,1)} async-done(((bf16[256,2,4,64]{3,2,1,0:T(4,128)(2,1)}), bf16[256,2,4,64]{3,2,1,0:T(4,128)(2,1)}) %all-reduce.7.cloned.1.call-update) | async-done | bytes 262160
  386.2 24.7 %all_to_all.142 = bf16[32,2,256]{2,1,0:T(2,128)(2,1)S(1)} all-to-all(bf16[32,2,256]{2,1,0:T(2,128)(2,1)S(1)} %reshape.134), channel_id=1, replica_groups=mesh['freq'=32,'rec'=8] {'freq'}, dimensions={0} | all-to-all | bytes 65536 | tf_op jit(solution)/shard_map/all_to_all | solution.py:74
  411.9 12.8 %all_to_all.143 = bf16[32,2,256]{2,1,0:T(2,128)(2,1)S(1)} all-to-all(bf16[32,2,256]{2,1,0:T(2,128)(2,1)S(1)} %reshape.136), channel_id=1, replica_groups=mesh['freq'=32,'rec'=8] {'freq'}, dimensions={0} | all-to-all | bytes 65536 | tf_op jit(solution)/shard_map/all_to_all | solution.py:81
  425.1 24.5 %all_gather.7 = bf16[256,2,4,64]{3,2,1,0:T(4,128)(2,1)S(1)} all-gather(bf16[32,2,4,64]{3,2,1,0:T(4,128)(2,1)S(1)} %copy.78), channel_id=1, replica_groups=mesh['freq'=32,'rec'=8] {'rec'}, dimensions={0}, use_global_device_ids=true | all-gather | bytes 294912 | tf_op jit(solution)/shard_map/all_gather | solution.py:82
  458.6 41.4 %all_to_all.144 = bf16[2,4,64,1152]{3,1,0,2:T(4,128)(2,1)S(1)} all-to-all(bf16[2,4,64,1152]{3,1,0,2:T(4,128)(2,1)S(1)} %copy.81), channel_id=1, replica_groups=mesh['freq'=32,'rec'=8] {'freq'}, dimensions={2} | all-to-all | bytes 2359296 | tf_op jit(solution)/shard_map/all_to_all | solution.py:84
  500.9 3.8 fusion.1
  (95 shorter events, 35.4 us)
Async XLA Ops:
  7.2 152.8 %copy-start = (s32[2,256]{1,0:T(2,128)S(1)}, s32[2,256]{1,0:T(2,128)}, u32[]{:S(2)}) copy-start(s32[2,256]{1,0:T(2,128)} %param.6) | copy-start | bytes 6148
  7.2 135.7 %all-reduce.5.cloned.1.call-start = ((), (), s32[]{:S(2)}) async-start(), calls=%async_computation.8 | async-start | bytes 1048576
  60.6 9.0 %slice-start = ((s8[4718592]{0:T(1024)(128)(4,1)}), s8[524288]{0:T(1024)(128)(4,1)S(1)}, s32[]{:S(2)}) async-start(s8[4718592]{0:T(1024)(128)(4,1)} %bitcast.235), calls=%async_computation.10 | async-start | bytes 1048576
  61.9 7.7 %slice-start.1 = ((s8[4718592]{0:T(1024)(128)(4,1)}), s8[4194304]{0:T(1024)(128)(4,1)S(1)}, s32[]{:S(2)}) async-start(s8[4718592]{0:T(1024)(128)(4,1)} %bitcast.235), calls=%async_computation.11 | async-start | bytes 8388608
  69.6 2.0 copy-start.3
  144.6 24.9 %all-to-all-start.1 = ((bf16[32,2,256]{2,1,0:T(2,128)(2,1)}), bf16[32,2,256]{2,1,0:T(2,128)(2,1)S(1)}, u32[]{:S(2)}, u32[]{:S(2)}) async-start(bf16[32,2,256]{2,1,0:T(2,128)(2,1)} %reshape.130), calls=%async_computation.1 | async-start | bytes 65536 | tf_op jit(solution)/shard_map/all_to_all | solution.py:74
  159.9 225.2 %all-reduce.7.cloned.1.call-start = ((), (), s32[]{:S(2)}) async-start(), calls=%async_computation.9 | async-start | bytes 1048576
  208.8 6.7 %slice-start.2 = ((s8[4718592]{0:T(1024)(128)(4,1)}), s8[4194304]{0:T(1024)(128)(4,1)S(1)}, s32[]{:S(2)}) async-start(s8[4718592]{0:T(1024)(128)(4,1)} %bitcast.237), calls=%async_computation.12 | async-start | bytes 8388608
  211.2 4.4 slice-start.3
  217.1 42.4 %copy-start.1 = (s32[2,1152]{1,0:T(2,128)S(1)}, s32[2,1152]{1,0:T(2,128)}, u32[]{:S(2)}) copy-start(s32[2,1152]{1,0:T(2,128)} %param.7) | copy-start | bytes 27652
  411.3 38.8 %copy-start.2 = (bf16[2,32,1024]{2,1,0:T(8,128)(2,1)}, bf16[2,32,1024]{2,1,0:T(8,128)(2,1)S(1)}, u32[]{:S(2)}) copy-start(bf16[2,32,1024]{2,1,0:T(8,128)(2,1)S(1)} %convolution_bitcast_fusion) | copy-start | bytes 393220
  450.1 6.9 %slice-start.4 = ((s8[4718592]{0:T(1024)(128)(4,1)}), s8[4194304]{0:T(1024)(128)(4,1)S(1)}, s32[]{:S(2)}) async-start(s8[4718592]{0:T(1024)(128)(4,1)} %bitcast.239), calls=%async_computation.14 | async-start | bytes 8388608
  452.4 4.6 slice-start.5
  454.7 46.2 %slice-start.6 = ((s8[4718592]{0:T(1024)(128)(4,1)}), s8[4194304]{0:T(1024)(128)(4,1)S(1)}, s32[]{:S(2)}) async-start(s8[4718592]{0:T(1024)(128)(4,1)} %bitcast.263), calls=%async_computation.16 | async-start | bytes 8388608
  457.5 43.4 %slice-start.7 = ((s8[4718592]{0:T(1024)(128)(4,1)}), s8[524288]{0:T(1024)(128)(4,1)S(1)}, s32[]{:S(2)}) async-start(s8[4718592]{0:T(1024)(128)(4,1)} %bitcast.263), calls=%async_computation.17 | async-start | bytes 1048576
Sparse Core Ops, SparseCore 0:
  71.7 71.0 all-reduce.4
  316.0 68.9 all-reduce.6
where the time goes:
time: 512 us
  blocking collectives  264 us (52%)
  waiting for transfers between devices  149 us (29%)
  matrix products  46.9 us (9%)
  local copies, waits for them, and re-layouts  18.7 us (4%)
  between operations  15.4 us (3%)
  starting transfers between devices  15.3 us (3%)
    unnamed x4, waiting for transfers between devices  139 us
    all_to_all x2, blocking collectives, body(): lax.all_to_all(reflected, 'freq', split_axis=2, concat_axis=1, tiled=True)  82.8 us
    all_to_all x2, blocking collectives, body(): lax.all_to_all(spectrum, 'freq', split_axis=1, concat_axis=2, tiled=True)  81.6 us
    all_gather x2, blocking collectives, body(): lax.all_gather(returned_output, 'rec', axis=0, tiled=True)  49.2 us
    all_to_all x2, blocking collectives, body(): lax.all_to_all(echo, 'freq', split_axis=2, concat_axis=3, tiled=True)  25.5 us
    all_to_all x1, blocking collectives, body(): lax.all_to_all(local, 'freq', split_axis=3, concat_axis=2, tiled=True)  24.7 us
    all_to_all x1, starting transfers between devices, body(): lax.all_to_all(local, 'freq', split_axis=3, concat_axis=2, tiled=True)  15.2 us
  transfers between devices with their start and end apart: 3, of which 3 were waited for; matrix products, arithmetic and copies ran while one was open for 0% of the time, Pallas kernels for 0%

commit v1 on v0

--- a/solution.py
+++ b/solution.py
@@ -79,7 +79,13 @@
             "pst,ckt->sckp", muted, forward, preferred_element_type=jnp.float32
         ).astype(jnp.bfloat16)
         returned_output = lax.all_to_all(echo, "freq", split_axis=2, concat_axis=3, tiled=True)
-        reflected = adjoint_mdc(kernel, lax.all_gather(returned_output, "rec", axis=0, tiled=True))
+        reflected = adjoint_mdc(
+            kernel,
+            jnp.concatenate(
+                lax.all_to_all(jnp.stack([returned_output] * lax.axis_size("rec")), "rec", 0, 0),
+                axis=0,
+            ),
+        )
         reflected = reflected.astype(jnp.bfloat16)
         arrived = lax.all_to_all(reflected, "freq", split_axis=2, concat_axis=1, tiled=True)
         update = jnp.einsum("ckpr,ckt->prt", arrived, inverse, preferred_element_type=jnp.float32)

time: 512 us -> 471 us (0.920)
  blocking collectives: 264 us -> 224 us
    all_gather x2 -> x0, blocking collectives: 49.2 us -> none  [body(): lax.all_gather(returned_output, 'rec', axis=0, tiled=True)]
    all_to_all x0 -> x2, blocking collectives: none -> 18.8 us  [body(): lax.all_to_all(jnp.stack([returned_output] * lax.axis_size('rec')), 'rec'...]
    all_to_all x2, blocking collectives: 82.8 us -> 73.6 us  [body(): lax.all_to_all(reflected, 'freq', split_axis=2, concat_axis=1, tiled=True)]
where the time goes in v1:
time: 471 us; the launch traced here: 470 us
  blocking collectives  224 us (48%)
  waiting for transfers between devices  149 us (32%)
  matrix products  43.6 us (9%)
  local copies, waits for them, and re-layouts  19.5 us (4%)
  between operations  15.4 us (3%)
  starting transfers between devices  15.3 us (3%)
    unnamed x4, waiting for transfers between devices  140 us
    all_to_all x2, blocking collectives, body(): lax.all_to_all(spectrum, 'freq', split_axis=1, concat_axis=2, tiled=True)  81.6 us
    all_to_all x2, blocking collectives, body(): lax.all_to_all(reflected, 'freq', split_axis=2, concat_axis=1, tiled=True)  73.6 us
    all_to_all x2, blocking collectives, body(): lax.all_to_all(echo, 'freq', split_axis=2, concat_axis=3, tiled=True)  25.5 us
    all_to_all x1, blocking collectives, body(): lax.all_to_all(local, 'freq', split_axis=3, concat_axis=2, tiled=True)  24.7 us
    all_to_all x2, blocking collectives, body(): lax.all_to_all(jnp.stack([returned_output] * lax.axis_size('rec')), 'rec'...  18.8 us
    all_to_all x1, starting transfers between devices, body(): lax.all_to_all(local, 'freq', split_axis=3, concat_axis=2, tiled=True)  15.2 us
    all_to_all x1, waiting for transfers between devices, body(): lax.all_to_all(local, 'freq', split_axis=3, concat_axis=2, tiled=True)  9.49 us
  transfers between devices with their start and end apart: 3, of which 3 were waited for; matrix products, arithmetic and copies ran while one was open for 0% of the time, Pallas kernels for 0%

profile of v1, /device:TPU:1, one launch (start us, length us, event | category | flops | bytes accessed | tf_op | source)
XLA Modules:
  0.0 469.7 jit_solution(17149706731501196605)
XLA Ops:
  7.2 2.4 cosine_convert_fusion
  9.7 3.8 fusion.6
  14.7 45.1 %all_to_all.142 = bf16[2,128,2,1152]{3,2,0,1:T(2,128)(2,1)S(1)} all-to-all(bf16[2,128,2,1152]{3,2,0,1:T(2,128)(2,1)S(1)} %copy.32), channel_id=1, replica_groups=mesh['freq'=32,'rec'=8] {'freq'}, dimensions={1} | all-to-all | bytes 2359296 | tf_op jit(solution)/shard_map/all_to_all | solution.py:65
  61.9 2.6 fusion.30
  64.6 2.5 fusion.28
  67.1 2.5 fusion.78
  72.9 70.0 %all-reduce.5.cloned.1.call-done = bf16[256,2,4,64]{3,2,1,0:T(4,128)(2,1)} async-done(((bf16[256,2,4,64]{3,2,1,0:T(4,128)(2,1)}), bf16[256,2,4,64]{3,2,1,0:T(4,128)(2,1)}) %all-reduce.5.cloned.1.call-update) | async-done | bytes 262160
  144.6 15.2 %all-to-all-start.1 = ((bf16[32,2,256]{2,1,0:T(2,128)(2,1)}), bf16[32,2,256]{2,1,0:T(2,128)(2,1)S(1)}, u32[]{:S(2)}, u32[]{:S(2)}) async-start(bf16[32,2,256]{2,1,0:T(2,128)(2,1)} %reshape.144), calls=%async_computation.1 | async-start | bytes 65536 | tf_op jit(solution)/shard_map/all_to_all | solution.py:74
  160.0 9.5 %all-to-all-done.1 = bf16[32,2,256]{2,1,0:T(2,128)(2,1)S(1)} async-done(((bf16[32,2,256]{2,1,0:T(2,128)(2,1)}), bf16[32,2,256]{2,1,0:T(2,128)(2,1)S(1)}, u32[]{:S(2)}, u32[]{:S(2)}) %all-to-all-start.1) | async-done | bytes 32800 | tf_op jit(solution)/shard_map/all_to_all | solution.py:74
  170.4 12.8 %all_to_all.143 = bf16[32,2,256]{2,1,0:T(2,128)(2,1)S(1)} all-to-all(bf16[32,2,256]{2,1,0:T(2,128)(2,1)S(1)} %reshape.146), channel_id=1, replica_groups=mesh['freq'=32,'rec'=8] {'freq'}, dimensions={0} | all-to-all | bytes 65536 | tf_op jit(solution)/shard_map/all_to_all | solution.py:81
  184.1 9.4 %all_to_all.144 = bf16[8,2,8192]{2,1,0:T(2,128)(2,1)S(1)} all-to-all(bf16[8,2,8192]{2,1,0:T(2,128)(2,1)S(1)} %reshape.148), channel_id=1, replica_groups=mesh['freq'=32,'rec'=8] {'rec'}, dimensions={0} | all-to-all | bytes 524288 | tf_op jit(solution)/shard_map/all_to_all | solution.py:85
  200.6 36.8 %all_to_all.145 = bf16[2,4,64,1152]{3,1,0,2:T(4,128)(2,1)S(1)} all-to-all(bf16[2,4,64,1152]{3,1,0,2:T(4,128)(2,1)S(1)} %copy.45), channel_id=1, replica_groups=mesh['freq'=32,'rec'=8] {'freq'}, dimensions={2} | all-to-all | bytes 2359296 | tf_op jit(solution)/shard_map/all_to_all | solution.py:90
  238.3 5.4 %fusion.9 = bf16[2,128,2,1152]{3,1,2,0:T(8,128)(2,1)S(1)} fusion(bf16[2,1152,1024]{2,1,0:T(8,128)(2,1)} %param.5, s32[2,1152]{1,0:T(2,128)S(1)} %copy-done.1, bf16[2,128,2,1152]{3,2,1,0:T(2,128)(2,1)S(1)} %bitcast.270, bf16[1,128,1024]{2,1,0:T(8,128)(2,1)S(1)} %get-tuple-element.7, bf16[1,128,1024]{2,1,0:T(8,128)(2,1)S(1)} %get-tuple-element.6), kind=kOutput, calls=%fused_computation.12 | convolution fusion | flops 2430402560 | bytes 7611392 | tf_op jit(solution)/shard_map/prt,ckt->ckpr/dot_general | solution.py:62
  245.0 36.5 %all_to_all.146 = bf16[2,128,2,1152]{3,2,0,1:T(2,128)(2,1)S(1)} all-to-all(bf16[2,128,2,1152]{3,2,0,1:T(2,128)(2,1)S(1)} %copy.48), channel_id=1, replica_groups=mesh['freq'=32,'rec'=8] {'freq'}, dimensions={1} | all-to-all | bytes 2359296 | tf_op jit(solution)/shard_map/all_to_all | solution.py:65
  283.3 2.5 fusion.24
  286.1 2.5 fusion.22
  288.6 2.5 fusion.84
  291.1 2.5 fusion.87
  294.8 69.5 %all-reduce.7.cloned.1.call-done = bf16[256,2,4,64]{3,2,1,0:T(4,128)(2,1)} async-done(((bf16[256,2,4,64]{3,2,1,0:T(4,128)(2,1)}), bf16[256,2,4,64]{3,2,1,0:T(4,128)(2,1)}) %all-reduce.7.cloned.1.call-update) | async-done | bytes 262160
  365.4 24.7 %all_to_all.147 = bf16[32,2,256]{2,1,0:T(2,128)(2,1)S(1)} all-to-all(bf16[32,2,256]{2,1,0:T(2,128)(2,1)S(1)} %reshape.150), channel_id=1, replica_groups=mesh['freq'=32,'rec'=8] {'freq'}, dimensions={0} | all-to-all | bytes 65536 | tf_op jit(solution)/shard_map/all_to_all | solution.py:74
  391.1 12.8 %all_to_all.148 = bf16[32,2,256]{2,1,0:T(2,128)(2,1)S(1)} all-to-all(bf16[32,2,256]{2,1,0:T(2,128)(2,1)S(1)} %reshape.152), channel_id=1, replica_groups=mesh['freq'=32,'rec'=8] {'freq'}, dimensions={0} | all-to-all | bytes 65536 | tf_op jit(solution)/shard_map/all_to_all | solution.py:81
  404.8 9.4 %all_to_all.149 = bf16[8,2,8192]{2,1,0:T(2,128)(2,1)S(1)} all-to-all(bf16[8,2,8192]{2,1,0:T(2,128)(2,1)S(1)} %reshape.154), channel_id=1, replica_groups=mesh['freq'=32,'rec'=8] {'rec'}, dimensions={0} | all-to-all | bytes 524288 | tf_op jit(solution)/shard_map/all_to_all | solution.py:85
  421.3 36.8 %all_to_all.150 = bf16[2,4,64,1152]{3,1,0,2:T(4,128)(2,1)S(1)} all-to-all(bf16[2,4,64,1152]{3,1,0,2:T(4,128)(2,1)S(1)} %copy.61), channel_id=1, replica_groups=mesh['freq'=32,'rec'=8] {'freq'}, dimensions={2} | all-to-all | bytes 2359296 | tf_op jit(solution)/shard_map/all_to_all | solution.py:90
  459.1 3.8 fusion.1
  (97 shorter events, 32.9 us)
Async XLA Ops:
  7.2 152.8 %copy-start = (s32[2,256]{1,0:T(2,128)S(1)}, s32[2,256]{1,0:T(2,128)}, u32[]{:S(2)}) copy-start(s32[2,256]{1,0:T(2,128)} %param.6) | copy-start | bytes 6148
  7.2 135.7 %all-reduce.5.cloned.1.call-start = ((), (), s32[]{:S(2)}) async-start(), calls=%async_computation.10 | async-start | bytes 1048576
  60.6 9.0 %slice-start = ((s8[4718592]{0:T(1024)(128)(4,1)}), s8[524288]{0:T(1024)(128)(4,1)S(1)}, s32[]{:S(2)}) async-start(s8[4718592]{0:T(1024)(128)(4,1)} %bitcast.247), calls=%async_computation.12 | async-start | bytes 1048576
  61.9 7.7 %slice-start.1 = ((s8[4718592]{0:T(1024)(128)(4,1)}), s8[4194304]{0:T(1024)(128)(4,1)S(1)}, s32[]{:S(2)}) async-start(s8[4718592]{0:T(1024)(128)(4,1)} %bitcast.247), calls=%async_computation.13 | async-start | bytes 8388608
  69.6 2.0 copy-start.3
  144.6 24.9 %all-to-all-start.1 = ((bf16[32,2,256]{2,1,0:T(2,128)(2,1)}), bf16[32,2,256]{2,1,0:T(2,128)(2,1)S(1)}, u32[]{:S(2)}, u32[]{:S(2)}) async-start(bf16[32,2,256]{2,1,0:T(2,128)(2,1)} %reshape.144), calls=%async_computation.1 | async-start | bytes 65536 | tf_op jit(solution)/shard_map/all_to_all | solution.py:74
  159.9 204.4 %all-reduce.7.cloned.1.call-start = ((), (), s32[]{:S(2)}) async-start(), calls=%async_computation.11 | async-start | bytes 1048576
  193.8 4.6 slice-start.2
  193.9 4.6 slice-start.3
  200.6 37.7 %copy-start.1 = (s32[2,1152]{1,0:T(2,128)S(1)}, s32[2,1152]{1,0:T(2,128)}, u32[]{:S(2)}) copy-start(s32[2,1152]{1,0:T(2,128)} %param.7) | copy-start | bytes 27652
  390.5 24.0 %copy-start.2 = (bf16[2,32,1024]{2,1,0:T(8,128)(2,1)}, bf16[2,32,1024]{2,1,0:T(8,128)(2,1)S(1)}, u32[]{:S(2)}) copy-start(bf16[2,32,1024]{2,1,0:T(8,128)(2,1)S(1)} %convolution_bitcast_fusion) | copy-start | bytes 393220
  414.2 5.0 %slice-start.4 = ((s8[4718592]{0:T(1024)(128)(4,1)}), s8[524288]{0:T(1024)(128)(4,1)S(1)}, s32[]{:S(2)}) async-start(s8[4718592]{0:T(1024)(128)(4,1)} %bitcast.251), calls=%async_computation.16 | async-start | bytes 1048576
  414.6 4.6 slice-start.5
  419.1 39.9 %slice-start.6 = ((s8[4718592]{0:T(1024)(128)(4,1)}), s8[4194304]{0:T(1024)(128)(4,1)S(1)}, s32[]{:S(2)}) async-start(s8[4718592]{0:T(1024)(128)(4,1)} %bitcast.285), calls=%async_computation.18 | async-start | bytes 8388608
  420.3 38.8 %slice-start.7 = ((s8[4718592]{0:T(1024)(128)(4,1)}), s8[524288]{0:T(1024)(128)(4,1)S(1)}, s32[]{:S(2)}) async-start(s8[4718592]{0:T(1024)(128)(4,1)} %bitcast.285), calls=%async_computation.19 | async-start | bytes 1048576
Sparse Core Ops, SparseCore 0:
  71.7 71.0 all-reduce.4
  294.9 69.3 all-reduce.6
